TPU v7x, 128 devices: a whole 4x4x4 slice. The times are simulated.
128 devices in a mesh: dp: 8 (over y, x_hi), section: 4 (over x_lo, core), mp: 4 (over z).
Axes of the slice: x: 4 (x_hi: 2, x_lo: 2; x = x_hi * 2 + x_lo), y: 4, z: 4, core: 2. Of those that a mesh axis runs over, the one named last changes fastest.
Arguments:
- hidden_in: bfloat16 [16, 128, 4096], P('dp')
- slot_hidden: bfloat16 [4, 16, 16, 4096], P('section', 'dp'), may hold values from -6 to 6
- norm_gain: float32 [4, 4096], P('section'), may hold values from 0.5 to 1.5
- w_query: bfloat16 [4, 4096, 3072], P('section', None, 'mp')
- w_key: bfloat16 [4, 4096, 1024], P('section', None, 'mp')
- w_value: bfloat16 [4, 4096, 1024], P('section', None, 'mp'), may hold values from -0.09375 to 0.09375
- w_out: bfloat16 [4, 3072, 4096], P('section', 'mp'), may hold values from -0.109375 to 0.109375
- key_a: bfloat16 [4, 4096, 64], P('section'), may hold values from -0.09375 to 0.09375
- key_b: bfloat16 [4, 64, 1024], P('section', None, 'mp'), may hold values from -0.375 to 0.375
- value_a: bfloat16 [4, 4096, 64], P('section'), may hold values from -0.09375 to 0.09375
- value_b: bfloat16 [4, 64, 1024], P('section', None, 'mp'), may hold values from -0.375 to 0.375
- cotangent: bfloat16 [16, 128, 4096], P('dp'), may hold values from -6 to 6
Outputs:
- grad_a: float32 [4, 2, 4096, 64], P('section')
- grad_b: float32 [4, 2, 64, 1024], P('section', None, None, 'mp')
All inputs are finite; a program needn't handle non-finite values.
Results may differ from a plain program's by a relative error of at most 0.028.
Values may be sent and summed in bfloat16 or wider, within the bound.
No kernel may reach another device: no remote copies, remote signals or barrier semaphores. Data moves between devices by JAX's collectives and lax.ppermute only.
A program may use at most 128 MiB of HBM per device.

v0:
```python
import math
import jax
import jax.numpy as jnp
from jax import lax
from jax.sharding import PartitionSpec as P

HD = 128
SLOTS = 16
MICRO = 2
EPS = 1e-05
NEG = -1e30
HIGH = lax.Precision.HIGHEST


def in_blocks(array, dim, length):
    before, after = (array.shape[:dim], array.shape[dim + 1 :])
    return jnp.moveaxis(array.reshape(*before, length, -1, *after), dim, 0)


def summed_on_arrival(array, axis, dim):
    length = lax.axis_size(axis)
    pieces = lax.all_to_all(in_blocks(array, dim, length), axis, 0, 0, tiled=True)
    return jnp.sum(pieces, axis=0)


def laid_out(pieces, dim):
    shape = list(pieces.shape[1:])
    shape[dim] *= pieces.shape[0]
    return jnp.moveaxis(pieces, 0, dim).reshape(shape)


def copy_for_each(array, axis):
    copies = jnp.broadcast_to(array, (lax.axis_size(axis), *array.shape))
    return lax.all_to_all(copies, axis, split_axis=0, concat_axis=0, tiled=True)


def collect(array, axis, dim):
    return laid_out(copy_for_each(array, axis), dim)


def passed_along(block, axis, distance):
    devices = range(lax.axis_size(axis))
    route = [(i - distance, i) for i in devices if i - distance in devices]
    return lax.ppermute(block, axis, route)


def sent_and_summed(array, axis, dim):
    pieces = in_blocks(array, dim, lax.axis_size(axis))
    arrived = lax.all_to_all(pieces, axis, split_axis=0, concat_axis=0, tiled=True)
    return arrived.astype(jnp.float32).sum(axis=0)


def taken_together(array, axis):
    everything = copy_for_each(array, axis)
    return jnp.sum(everything, axis=0)


def normalize(rows):
    wide = rows.astype(jnp.float32)
    inverse = lax.rsqrt(jnp.mean(wide * wide, axis=-1, keepdims=True) + EPS)
    return (wide * inverse, inverse)


def visible(count, slots):
    qpos = lax.broadcasted_iota(jnp.int32, (count, slots + count), 0)
    kpos = lax.broadcasted_iota(jnp.int32, (count, slots + count), 1)
    return (kpos < slots) | (kpos - slots <= qpos)


def mixdot(left, right):
    return jnp.dot(left, right, preferred_element_type=jnp.float32)


def attend(query, keys, values):
    count = query.shape[0]
    groups = keys.shape[1] // HD
    per_group = query.shape[1] // keys.shape[1]
    q_four = query.reshape(count, groups, per_group, HD)
    k_three = keys.reshape(-1, groups, HD)
    v_three = values.reshape(-1, groups, HD)
    scores = jnp.einsum(
        "igcd,jgd->gcij", q_four, k_three, preferred_element_type=jnp.float32
    ) / math.sqrt(HD)
    scores = jnp.where(visible(count, SLOTS), scores, NEG)
    top = jnp.max(scores, axis=-1, keepdims=True)
    probs = jnp.exp(scores - top)
    probs = probs / jnp.sum(probs, axis=-1, keepdims=True)
    weights = probs.astype(jnp.bfloat16)
    mixed = jnp.einsum("gcij,jgd->igcd", weights, v_three, preferred_element_type=jnp.float32)
    return (mixed.reshape(count, -1).astype(jnp.bfloat16), probs, weights)


def attend_back(grad_mixed, query, keys, values, probs, weights):
    count = query.shape[0]
    groups = keys.shape[1] // HD
    per_group = query.shape[1] // keys.shape[1]
    q_four = query.reshape(count, groups, per_group, HD)
    k_three = keys.reshape(-1, groups, HD)
    v_three = values.reshape(-1, groups, HD)
    g_four = grad_mixed.reshape(count, groups, per_group, HD)
    grad_probs = jnp.einsum("igcd,jgd->gcij", g_four, v_three, preferred_element_type=jnp.float32)
    grad_values = jnp.einsum("gcij,igcd->jgd", weights, g_four, preferred_element_type=jnp.float32)
    grad_scores = probs * (grad_probs - jnp.sum(probs * grad_probs, axis=-1, keepdims=True))
    scaled = (grad_scores / math.sqrt(HD)).astype(jnp.bfloat16)
    grad_query = jnp.einsum("gcij,jgd->igcd", scaled, k_three, preferred_element_type=jnp.float32)
    grad_keys = jnp.einsum("gcij,igcd->jgd", scaled, q_four, preferred_element_type=jnp.float32)
    return (
        grad_query.reshape(count, -1).astype(jnp.bfloat16),
        grad_keys.reshape(-1, groups * HD),
        grad_values.reshape(-1, groups * HD),
    )


def slot_entries(slot_rows, gain, w_key, w_value, key_a, key_b, value_a, value_b):
    unit, inverse = normalize(slot_rows)
    slot_normed = (unit * gain).astype(jnp.bfloat16)
    low_key = mixdot(slot_normed, key_a).astype(jnp.bfloat16)
    low_value = mixdot(slot_normed, value_a).astype(jnp.bfloat16)
    slot_keys = (mixdot(slot_normed, w_key) + mixdot(low_key, key_b)).astype(jnp.bfloat16)
    slot_values = (mixdot(slot_normed, w_value) + mixdot(low_value, value_b)).astype(jnp.bfloat16)
    return (slot_normed, low_key, low_value, slot_keys, slot_values)


def local(
    hidden_in,
    slot_hidden,
    norm_gain,
    w_query,
    w_key,
    w_value,
    w_out,
    key_a,
    key_b,
    value_a,
    value_b,
    cotangent,
):
    gain = norm_gain[0]
    w_q = w_query[0]
    w_k = w_key[0]
    w_v = w_value[0]
    w_o = w_out[0]
    down_key = key_a[0]
    up_key = key_b[0]
    down_value = value_a[0]
    up_value = value_b[0]
    slot_all = slot_hidden[0]
    section = lax.axis_index("section")
    sections = lax.axis_size("section")
    ticks = MICRO + sections - 1
    first = section == 0
    final = section == sections - 1
    block_rows = hidden_in.shape[1]
    share = block_rows // lax.axis_size("mp")
    offset = lax.axis_index("mp") * share

    def project_all(normed):
        return (
            mixdot(normed, w_q).astype(jnp.bfloat16),
            mixdot(normed, w_k).astype(jnp.bfloat16),
            mixdot(normed, w_v).astype(jnp.bfloat16),
        )

    def attention_core(normed, slot_rows):
        query, key_tok, value_tok = project_all(normed)
        slot_normed, low_key, low_value, slot_keys, slot_values = slot_entries(
            slot_rows, gain, w_k, w_v, down_key, up_key, down_value, up_value
        )
        keys = jnp.concatenate([slot_keys, key_tok], axis=0)
        values = jnp.concatenate([slot_values, value_tok], axis=0)
        mixed, probs, weights = attend(query, keys, values)
        return (query, keys, values, mixed, probs, weights, slot_normed, low_key, low_value)

    arrive = jnp.zeros_like(hidden_in[0])
    kept_rows = jnp.zeros_like(hidden_in)
    for tick in range(ticks):
        micro = tick - section
        valid = (micro >= 0) & (micro < MICRO)
        place = jnp.clip(micro, 0, MICRO - 1)
        rows = jnp.where(first, hidden_in[min(tick, MICRO - 1)], arrive)
        kept_rows = jnp.where(
            valid, lax.dynamic_update_index_in_dim(kept_rows, rows, place, 0), kept_rows
        )
        unit, inverse = normalize(rows)
        normed = (unit * gain).astype(jnp.bfloat16)
        slot_rows = lax.dynamic_index_in_dim(slot_all, place, 0, keepdims=False)
        mixed = attention_core(normed, slot_rows)[3]
        summed = summed_on_arrival(mixdot(mixed, w_o), "mp", 0)
        own_rows = lax.dynamic_slice_in_dim(rows, offset, share, 0)
        own_result = (own_rows.astype(jnp.float32) + summed).astype(jnp.bfloat16)
        result = collect(own_result, "mp", 0)
        if tick + 1 < ticks:
            arrive = passed_along(result, "section", 1)
    grad_in = jnp.zeros((share, hidden_in.shape[2]), jnp.float32)
    sum_b = jnp.zeros((2,) + up_key.shape, jnp.float32)
    low_store = jnp.zeros((2, MICRO, SLOTS, up_key.shape[0]), jnp.float32)
    slot_store = jnp.zeros((MICRO, SLOTS, hidden_in.shape[2]), jnp.bfloat16)
    for tick in range(ticks):
        micro = tick - (sections - 1 - section)
        valid = (micro >= 0) & (micro < MICRO)
        place = jnp.clip(micro, 0, MICRO - 1)
        own_cot = lax.dynamic_slice_in_dim(cotangent[min(tick, MICRO - 1)], offset, share, 0)
        grad = jnp.where(final, own_cot.astype(jnp.float32), grad_in)
        rows = lax.dynamic_index_in_dim(kept_rows, place, 0, keepdims=False)
        unit, inverse = normalize(rows)
        normed = (unit * gain).astype(jnp.bfloat16)
        slot_rows = lax.dynamic_index_in_dim(slot_all, place, 0, keepdims=False)
        query, keys, values, mixed, probs, weights, slot_normed, low_key, low_value = (
            attention_core(normed, slot_rows)
        )
        grad_low = grad.astype(jnp.bfloat16)
        grad_mixed = mixdot(lax.all_gather(grad_low, "mp", axis=0, tiled=True), w_o.T).astype(
            jnp.bfloat16
        )
        grad_query, grad_keys, grad_values = attend_back(
            grad_mixed, query, keys, values, probs, weights
        )
        key_grad = grad_keys.astype(jnp.bfloat16)
        value_grad = grad_values.astype(jnp.bfloat16)
        total = mixdot(grad_query, w_q.T)
        total = total + mixdot(
            lax.dynamic_slice_in_dim(key_grad, SLOTS, share * lax.axis_size("mp"), 0), w_k.T
        )
        grad_normed = sent_and_summed(
            (
                total
                + mixdot(
                    lax.dynamic_slice_in_dim(value_grad, SLOTS, share * lax.axis_size("mp"), 0),
                    w_v.T,
                )
            ).astype(jnp.bfloat16),
            "mp",
            0,
        )
        own_unit = lax.dynamic_slice_in_dim(unit, offset, share, 0)
        own_inverse = lax.dynamic_slice_in_dim(inverse, offset, share, 0)
        scaled = grad_normed * gain
        grad_rows = grad + own_inverse * (
            scaled - own_unit * jnp.mean(scaled * own_unit, axis=-1, keepdims=True)
        )
        slot_key_grad = key_grad[:SLOTS]
        slot_value_grad = value_grad[:SLOTS]
        term_b = jnp.stack([mixdot(low_key.T, slot_key_grad), mixdot(low_value.T, slot_value_grad)])
        sum_b = sum_b + jnp.where(valid, term_b, 0.0)
        low_grads = jnp.stack(
            [mixdot(slot_key_grad, up_key.T), mixdot(slot_value_grad, up_value.T)]
        )
        low_store = jnp.where(
            valid, lax.dynamic_update_index_in_dim(low_store, low_grads, place, 1), low_store
        )
        slot_store = jnp.where(
            valid, lax.dynamic_update_index_in_dim(slot_store, slot_normed, place, 0), slot_store
        )
        if tick + 1 < ticks:
            grad_in = passed_along(grad_rows.astype(jnp.bfloat16), "section", -1).astype(
                grad_rows.dtype
            )
    low_total = taken_together(low_store, "mp")
    term = jnp.einsum("msd,tmsr->tdr", slot_store.astype(jnp.float32), low_total, precision=HIGH)
    grad_a, grad_b = (
        lax.psum(term.astype(jnp.bfloat16), "dp").astype(jnp.float32),
        lax.psum(sum_b.astype(jnp.bfloat16), "dp").astype(jnp.float32),
    )
    return (grad_a[None], grad_b[None])


def solution(mesh):
    placed = (
        P("dp", None, None),
        P("section", "dp", None, None),
        P("section", None),
        P("section", None, "mp"),
        P("section", None, "mp"),
        P("section", None, "mp"),
        P("section", "mp", None),
        P("section", None, None),
        P("section", None, "mp"),
        P("section", None, None),
        P("section", None, "mp"),
        P("dp", None, None),
    )
    return jax.shard_map(
        local,
        mesh=mesh,
        in_specs=placed,
        out_specs=(P("section", None, None, None), P("section", None, None, "mp")),
        check_vma=False,
    )
```

profile of v0, /device:TPU:0, one launch (start us, length us, event | category | flops | bytes accessed | tf_op | source)
XLA Modules:
  0.0 796.3 jit_solution(8733194437734446645)
XLA Ops:
  59.9 15.5 %all-to-all-done = f32[4,32,4096]{2,1,0:T(8,128)} async-done(((f32[4,32,4096]{2,1,0:T(8,128)}), f32[4,32,4096]{2,1,0:T(8,128)}, u32[]{:S(2)}, u32[]{:S(2)}) %all-to-all-start) | async-done | bytes 2097184 | tf_op jit(solution)/shard_map/all_to_all | solution.py:22
  88.3 10.4 %all-to-all-done.1 = bf16[4,32,4096]{2,1,0:T(8,128)(2,1)} async-done(((bf16[4,32,4096]{2,1,0:T(8,128)(2,1)}), bf16[4,32,4096]{2,1,0:T(8,128)(2,1)}, u32[]{:S(2)}, u32[]{:S(2)}) %all-to-all-start.1) | async-done | bytes 1048608 | tf_op jit(solution)/shard_map/all_to_all | solution.py:34
  133.0 15.4 %all-to-all-done.2 = f32[4,32,4096]{2,1,0:T(8,128)} async-done(((f32[4,32,4096]{2,1,0:T(8,128)}), f32[4,32,4096]{2,1,0:T(8,128)}, u32[]{:S(2)}, u32[]{:S(2)}) %all-to-all-start.2) | async-done | bytes 2097184 | tf_op jit(solution)/shard_map/all_to_all | solution.py:22
  160.6 7.3 all-to-all-done.3
  167.9 7.3 collective-permute-start.1
  199.4 21.6 %all-to-all-done.4 = f32[4,32,4096]{2,1,0:T(8,128)} async-done(((f32[4,32,4096]{2,1,0:T(8,128)}), f32[4,32,4096]{2,1,0:T(8,128)}, u32[]{:S(2)}, u32[]{:S(2)}) %all-to-all-start.4) | async-done | bytes 2097184 | tf_op jit(solution)/shard_map/all_to_all | solution.py:22
  230.2 11.7 %all-to-all-done.5 = bf16[4,32,4096]{2,1,0:T(8,128)(2,1)} async-done(((bf16[4,32,4096]{2,1,0:T(8,128)(2,1)}), bf16[4,32,4096]{2,1,0:T(8,128)(2,1)}, u32[]{:S(2)}, u32[]{:S(2)}) %all-to-all-start.5) | async-done | bytes 1048608 | tf_op jit(solution)/shard_map/all_to_all | solution.py:34
  241.9 6.5 collective-permute-start.2
  282.2 10.2 %all-to-all-done.6 = f32[4,32,4096]{2,1,0:T(8,128)} async-done(((f32[4,32,4096]{2,1,0:T(8,128)}), f32[4,32,4096]{2,1,0:T(8,128)}, u32[]{:S(2)}, u32[]{:S(2)}) %all-to-all-start.6) | async-done | bytes 2097184 | tf_op jit(solution)/shard_map/all_to_all | solution.py:22
  304.0 8.5 %all-to-all-done.7 = bf16[4,32,4096]{2,1,0:T(8,128)(2,1)} async-done(((bf16[4,32,4096]{2,1,0:T(8,128)(2,1)}), bf16[4,32,4096]{2,1,0:T(8,128)(2,1)}, u32[]{:S(2)}, u32[]{:S(2)}) %all-to-all-start.7) | async-done | bytes 1048608 | tf_op jit(solution)/shard_map/all_to_all | solution.py:34
  312.5 9.2 %collective-permute-start.3 = (bf16[128,4096]{1,0:T(8,128)(2,1)}, bf16[128,4096]{1,0:T(8,128)(2,1)S(1)}, u32[]{:S(2)}, u32[]{:S(2)}) collective-permute-start(bf16[128,4096]{1,0:T(8,128)(2,1)} %bitcast.43), channel_id=1, source_target_pairs={{0,4},{4,8},{8,12},{1,5},{5,9},{9,13},{2,6},{6,10},{10,14},{3,7},{... | collective-permute-start | bytes 3145736 | tf_op jit(solution)/shard_map/ppermute | solution.py:44
  345.5 6.3 fusion.44
  362.2 6.4 convert_bitcast_fusion
  376.5 7.7 collective-permute-done.4
  403.7 12.3 %all-gather.8.cloned.1.call-done = bf16[128,4096]{1,0:T(8,128)(2,1)} async-done(((bf16[32,4096]{1,0:T(8,128)(2,1)}), bf16[128,4096]{1,0:T(8,128)(2,1)}) %all-gather.8.cloned.1.call-update) | async-done | bytes 1048592 | tf_op jit(solution)/shard_map/all_gather | solution.py:212
  416.0 6.0 fusion.251
  432.7 6.5 fusion.40
  455.0 11.6 %all-to-all-done.9 = bf16[4,32,4096]{2,1,0:T(8,128)(2,1)} async-done(((bf16[4,32,4096]{2,1,0:T(8,128)(2,1)}), bf16[4,32,4096]{2,1,0:T(8,128)(2,1)}, u32[]{:S(2)}, u32[]{:S(2)}) %all-to-all-start.9) | async-done | bytes 1048608 | tf_op jit(solution)/shard_map/all_to_all | solution.py:49
  487.6 15.3 %all-gather.10.cloned.1.call-done = bf16[128,4096]{1,0:T(8,128)(2,1)} async-done(((bf16[32,4096]{1,0:T(8,128)(2,1)}), bf16[128,4096]{1,0:T(8,128)(2,1)}) %all-gather.10.cloned.1.call-update) | async-done | bytes 1048592 | tf_op jit(solution)/shard_map/all_gather | solution.py:212
  518.7 6.4 fusion.36
  574.9 8.2 %all-gather.12.cloned.1.call-done = bf16[128,4096]{1,0:T(8,128)(2,1)} async-done(((bf16[32,4096]{1,0:T(8,128)(2,1)}), bf16[128,4096]{1,0:T(8,128)(2,1)}) %all-gather.12.cloned.1.call-update) | async-done | bytes 1048592 | tf_op jit(solution)/shard_map/all_gather | solution.py:212
  599.7 6.4 fusion.32
  653.5 16.2 %all-gather.14.cloned.1.call-done = bf16[128,4096]{1,0:T(8,128)(2,1)} async-done(((bf16[32,4096]{1,0:T(8,128)(2,1)}), bf16[128,4096]{1,0:T(8,128)(2,1)}) %all-gather.14.cloned.1.call-update) | async-done | bytes 1048592 | tf_op jit(solution)/shard_map/all_gather | solution.py:212
  695.0 90.7 %all-reduce.3.cloned.1.call-done = (bf16[1,2,4096,64]{2,3,1,0:T(8,128)(2,1)}, bf16[1,2,64,256]{3,2,1,0:T(8,128)(2,1)}) async-done(((bf16[1,2,4096,64]{2,3,1,0:T(8,128)(2,1)}, bf16[1,2,64,256]{3,2,1,0:T(8,128)(2,1)}), (bf16[1,2,4096,64]{2,3,1,0:T(8,128)(2,1)}, bf16[1,2,64,256]{3,2,1,0:T(8,128)(2,1)})) %all-reduce.3.cloned.1.call-update) | async-done | bytes 1114128 | tf_op jit(solution)/shard_map/psum | solution.py:261
  (600 shorter events, 456.1 us)
Async XLA Ops:
  7.2 268.9 %all-gather.6.cloned.1.call-start = ((), (), s32[]{:S(2)}) async-start(), calls=%async_computation.13 | async-start | bytes 1310720 | tf_op jit(solution)/shard_map/all_gather | solution.py:212
  43.2 32.2 %all-to-all-start = ((f32[4,32,4096]{2,1,0:T(8,128)}), f32[4,32,4096]{2,1,0:T(8,128)}, u32[]{:S(2)}, u32[]{:S(2)}) async-start(f32[4,32,4096]{2,1,0:T(8,128)} %fusion.20), calls=%async_computation | async-start | bytes 4194304 | tf_op jit(solution)/shard_map/all_to_all | solution.py:22
  80.2 18.5 %all-to-all-start.1 = ((bf16[4,32,4096]{2,1,0:T(8,128)(2,1)}), bf16[4,32,4096]{2,1,0:T(8,128)(2,1)}, u32[]{:S(2)}, u32[]{:S(2)}) async-start(bf16[4,32,4096]{2,1,0:T(8,128)(2,1)} %broadcast_in_dim.174), calls=%async_computation.1 | async-start | bytes 2097152 | tf_op jit(solution)/shard_map/all_to_all | solution.py:34
  98.7 8.1 %collective-permute-start = (bf16[128,4096]{1,0:T(8,128)(2,1)}, bf16[128,4096]{1,0:T(8,128)(2,1)S(1)}, u32[]{:S(2)}, u32[]{:S(2)}) collective-permute-start(bf16[128,4096]{1,0:T(8,128)(2,1)} %bitcast.19), channel_id=1, source_target_pairs={{0,4},{4,8},{8,12},{1,5},{5,9},{9,13},{2,6},{6,10},{10,14},{3,7},{... | collective-permute-start | bytes 3145736 | tf_op jit(solution)/shard_map/ppermute | solution.py:44
  122.5 25.9 %all-to-all-start.2 = ((f32[4,32,4096]{2,1,0:T(8,128)}), f32[4,32,4096]{2,1,0:T(8,128)}, u32[]{:S(2)}, u32[]{:S(2)}) async-start(f32[4,32,4096]{2,1,0:T(8,128)} %fusion.18), calls=%async_computation.2 | async-start | bytes 4194304 | tf_op jit(solution)/shard_map/all_to_all | solution.py:22
  152.3 15.6 %all-to-all-start.3 = ((bf16[4,32,4096]{2,1,0:T(8,128)(2,1)}), bf16[4,32,4096]{2,1,0:T(8,128)(2,1)}, u32[]{:S(2)}, u32[]{:S(2)}) async-start(bf16[4,32,4096]{2,1,0:T(8,128)(2,1)} %broadcast_in_dim.176), calls=%async_computation.3 | async-start | bytes 2097152 | tf_op jit(solution)/shard_map/all_to_all | solution.py:34
  167.9 12.3 %collective-permute-start.1 = (bf16[128,4096]{1,0:T(8,128)(2,1)}, bf16[128,4096]{1,0:T(8,128)(2,1)S(1)}, u32[]{:S(2)}, u32[]{:S(2)}) collective-permute-start(bf16[128,4096]{1,0:T(8,128)(2,1)} %bitcast.27), channel_id=1, source_target_pairs={{0,4},{4,8},{8,12},{1,5},{5,9},{9,13},{2,6},{6,10},{10,14},{3,7},{... | collective-permute-start | bytes 3145736 | tf_op jit(solution)/shard_map/ppermute | solution.py:44
  194.6 26.5 %all-to-all-start.4 = ((f32[4,32,4096]{2,1,0:T(8,128)}), f32[4,32,4096]{2,1,0:T(8,128)}, u32[]{:S(2)}, u32[]{:S(2)}) async-start(f32[4,32,4096]{2,1,0:T(8,128)} %fusion.16), calls=%async_computation.4 | async-start | bytes 4194304 | tf_op jit(solution)/shard_map/all_to_all | solution.py:22
  225.9 16.1 %all-to-all-start.5 = ((bf16[4,32,4096]{2,1,0:T(8,128)(2,1)}), bf16[4,32,4096]{2,1,0:T(8,128)(2,1)}, u32[]{:S(2)}, u32[]{:S(2)}) async-start(bf16[4,32,4096]{2,1,0:T(8,128)(2,1)} %broadcast_in_dim.178), calls=%async_computation.5 | async-start | bytes 2097152 | tf_op jit(solution)/shard_map/all_to_all | solution.py:34
  241.9 8.9 %collective-permute-start.2 = (bf16[128,4096]{1,0:T(8,128)(2,1)}, bf16[128,4096]{1,0:T(8,128)(2,1)S(1)}, u32[]{:S(2)}, u32[]{:S(2)}) collective-permute-start(bf16[128,4096]{1,0:T(8,128)(2,1)} %bitcast.35), channel_id=1, source_target_pairs={{0,4},{4,8},{8,12},{1,5},{5,9},{9,13},{2,6},{6,10},{10,14},{3,7},{... | collective-permute-start | bytes 3145736 | tf_op jit(solution)/shard_map/ppermute | solution.py:44
  268.5 23.8 %all-to-all-start.6 = ((f32[4,32,4096]{2,1,0:T(8,128)}), f32[4,32,4096]{2,1,0:T(8,128)}, u32[]{:S(2)}, u32[]{:S(2)}) async-start(f32[4,32,4096]{2,1,0:T(8,128)} %fusion.14), calls=%async_computation.6 | async-start | bytes 4194304 | tf_op jit(solution)/shard_map/all_to_all | solution.py:22
  297.3 15.2 %all-to-all-start.7 = ((bf16[4,32,4096]{2,1,0:T(8,128)(2,1)}), bf16[4,32,4096]{2,1,0:T(8,128)(2,1)}, u32[]{:S(2)}, u32[]{:S(2)}) async-start(bf16[4,32,4096]{2,1,0:T(8,128)(2,1)} %broadcast_in_dim.180), calls=%async_computation.7 | async-start | bytes 2097152 | tf_op jit(solution)/shard_map/all_to_all | solution.py:34
  312.5 14.8 %collective-permute-start.3 = (bf16[128,4096]{1,0:T(8,128)(2,1)}, bf16[128,4096]{1,0:T(8,128)(2,1)S(1)}, u32[]{:S(2)}, u32[]{:S(2)}) collective-permute-start(bf16[128,4096]{1,0:T(8,128)(2,1)} %bitcast.43), channel_id=1, source_target_pairs={{0,4},{4,8},{8,12},{1,5},{5,9},{9,13},{2,6},{6,10},{10,14},{3,7},{... | collective-permute-start | bytes 3145736 | tf_op jit(solution)/shard_map/ppermute | solution.py:44
  356.6 14.4 %all-to-all-start.8 = ((bf16[4,32,4096]{2,1,0:T(8,128)(2,1)}), bf16[4,32,4096]{2,1,0:T(8,128)(2,1)S(1)}, u32[]{:S(2)}, u32[]{:S(2)}) async-start(bf16[4,32,4096]{2,1,0:T(8,128)(2,1)} %bitcast.1216), calls=%async_computation.8 | async-start | bytes 2097152 | tf_op jit(solution)/shard_map/all_to_all | solution.py:49
  360.1 55.9 %all-gather.8.cloned.1.call-start = ((), (), s32[]{:S(2)}) async-start(), calls=%async_computation.14 | async-start | bytes 1310720 | tf_op jit(solution)/shard_map/all_gather | solution.py:212
  373.8 10.5 %collective-permute-start.4 = (bf16[32,4096]{1,0:T(8,128)(2,1)S(1)}, bf16[32,4096]{1,0:T(8,128)(2,1)S(1)}, u32[]{:S(2)}, u32[]{:S(2)}) collective-permute-start(bf16[32,4096]{1,0:T(8,128)(2,1)S(1)} %fusion.489), channel_id=1, source_target_pairs={{4,0},{8,4},{12,8},{5,1},{9,5},{13,9},{6,2},{10,6},{14,10},{7,3},{... | collective-permute-start | bytes 786440 | tf_op jit(solution)/shard_map/ppermute | solution.py:44
  448.8 17.8 %all-to-all-start.9 = ((bf16[4,32,4096]{2,1,0:T(8,128)(2,1)}), bf16[4,32,4096]{2,1,0:T(8,128)(2,1)}, u32[]{:S(2)}, u32[]{:S(2)}) async-start(bf16[4,32,4096]{2,1,0:T(8,128)(2,1)} %bitcast.1217), calls=%async_computation.9 | async-start | bytes 2097152 | tf_op jit(solution)/shard_map/all_to_all | solution.py:49
  453.2 49.7 %all-gather.10.cloned.1.call-start = ((), (), s32[]{:S(2)}) async-start(), calls=%async_computation.15 | async-start | bytes 1310720 | tf_op jit(solution)/shard_map/all_gather | solution.py:212
  529.9 17.6 %all-to-all-start.10 = ((bf16[4,32,4096]{2,1,0:T(8,128)(2,1)}), bf16[4,32,4096]{2,1,0:T(8,128)(2,1)}, u32[]{:S(2)}, u32[]{:S(2)}) async-start(bf16[4,32,4096]{2,1,0:T(8,128)(2,1)} %bitcast.1215), calls=%async_computation.10 | async-start | bytes 2097152 | tf_op jit(solution)/shard_map/all_to_all | solution.py:49
  534.1 48.9 %all-gather.12.cloned.1.call-start = ((), (), s32[]{:S(2)}) async-start(), calls=%async_computation.16 | async-start | bytes 1310720 | tf_op jit(solution)/shard_map/all_gather | solution.py:212
  615.7 17.6 %all-to-all-start.11 = ((bf16[4,32,4096]{2,1,0:T(8,128)(2,1)}), bf16[4,32,4096]{2,1,0:T(8,128)(2,1)}, u32[]{:S(2)}, u32[]{:S(2)}) async-start(bf16[4,32,4096]{2,1,0:T(8,128)(2,1)} %bitcast.1214), calls=%async_computation.11 | async-start | bytes 2097152 | tf_op jit(solution)/shard_map/all_to_all | solution.py:49
  620.0 49.8 %all-gather.14.cloned.1.call-start = ((), (), s32[]{:S(2)}) async-start(), calls=%async_computation.17 | async-start | bytes 1310720 | tf_op jit(solution)/shard_map/all_gather | solution.py:212
  682.6 9.0 %all-to-all-start.12 = ((f32[4,1,4096]{2,1,0:T(1,128)}), f32[4,1,4096]{2,1,0:T(1,128)S(1)}, u32[]{:S(2)}, u32[]{:S(2)}) async-start(f32[4,1,4096]{2,1,0:T(1,128)} %reshape.1693), calls=%async_computation.12 | async-start | bytes 131072 | tf_op jit(solution)/shard_map/all_to_all | solution.py:34
  685.9 99.8 %all-reduce.3.cloned.1.call-start = ((), (), s32[]{:S(2)}) async-start(), calls=%async_computation.18 | async-start | bytes 2228224 | tf_op jit(solution)/shard_map/psum | solution.py:261
  (126 other events, 693.4 us)
Sparse Core Ops, SparseCore 0:
  11.1 26.8 all-gather.5
  385.9 30.0 all-gather.7
  475.8 27.0 all-gather.9
  556.4 26.6 all-gather.11
  644.2 25.5 all-gather.13
  695.2 90.5 all-reduce.2
where the time goes:
time: 808 us; the launch traced here: 796 us
  waiting for transfers between devices  281 us (35%)
  matrix products  277 us (34%)
  starting transfers between devices  87.2 us (11%)
  other arithmetic  78.6 us (10%)
  local copies, waits for them, and re-layouts  56.6 us (7%)
  between operations  16.3 us (2%)
    dot_general x114, matrix products, mixdot(): return jnp.dot(left, right, preferred_element_type=jnp.float32)  220 us
    psum x1, waiting for transfers between devices, local(): lax.psum(term.astype(jnp.bfloat16), 'dp').astype(jnp.float32)  90.7 us
    all_to_all x4, waiting for transfers between devices, summed_on_arrival(): lax.all_to_all(in_blocks(array, dim, length), axis, 0, 0, tiled=True)  62.7 us
    all_gather x5, waiting for transfers between devices, local(): lax.all_gather(grad_low, 'mp', axis=0, tiled=True)  52.1 us
    all_to_all x5, waiting for transfers between devices, copy_for_each(): return lax.all_to_all(copies, axis, split_axis=0, concat_axis=0, tiled=True)  42.8 us
    ppermute x8, starting transfers between devices, passed_along(): return lax.ppermute(block, axis, route)  30.8 us
    all_to_all x4, waiting for transfers between devices, sent_and_summed(): lax.all_to_all(pieces, axis, split_axis=0, concat_axis=0, tiled=True)  23 us
    all_to_all x5, starting transfers between devices, copy_for_each(): return lax.all_to_all(copies, axis, split_axis=0, concat_axis=0, tiled=True)  20.5 us
  transfers between devices with their start and end apart: 27, of which 21 were waited for; matrix products, arithmetic and copies ran while one was open for 30% of the time, Pallas kernels for 0%

commit v1 on v0

--- a/solution.py
+++ b/solution.py
@@ -3,6 +3,7 @@
 import jax.numpy as jnp
 from jax import lax
 from jax.sharding import PartitionSpec as P
+from jax.lax import all_gather
 
 HD = 128
 SLOTS = 16
@@ -257,8 +258,9 @@
             )
     low_total = taken_together(low_store, "mp")
     term = jnp.einsum("msd,tmsr->tdr", slot_store.astype(jnp.float32), low_total, precision=HIGH)
+    time_the_terms = lambda x0: jnp.sum(all_gather(x0, "dp"), 0)
     grad_a, grad_b = (
-        lax.psum(term.astype(jnp.bfloat16), "dp").astype(jnp.float32),
+        time_the_terms(term.astype(jnp.bfloat16)).astype(jnp.float32),
         lax.psum(sum_b.astype(jnp.bfloat16), "dp").astype(jnp.float32),
     )
     return (grad_a[None], grad_b[None])

time: 808 us -> 907 us (1.12)
  waiting for transfers between devices: 281 us -> 377 us
    all_gather x0 -> x1, waiting for transfers between devices: none -> 106 us  [local(): time_the_terms = lambda x0: jnp.sum(all_gather(x0, 'dp'), 0)]
    psum x1, waiting for transfers between devices: 90.7 us -> 79.7 us  [local(): lax.psum(sum_b.astype(jnp.bfloat16), 'dp').astype(jnp.float32)]
  transfers between devices with their start and end apart: 27 -> 28, of which waited for: 21 -> 22; matrix products, arithmetic and copies ran while one was open for 30% -> 27% of each run, Pallas kernels for 0% -> 0%
where the time goes in v1:
time: 907 us; the launch traced here: 895 us
  waiting for transfers between devices  377 us (42%)
  matrix products  275 us (30%)
  starting transfers between devices  87.6 us (10%)
  other arithmetic  83.2 us (9%)
  local copies, waits for them, and re-layouts  56.5 us (6%)
  between operations  16.3 us (2%)
    dot_general x114, matrix products, mixdot(): return jnp.dot(left, right, preferred_element_type=jnp.float32)  218 us
    all_gather x1, waiting for transfers between devices, local(): time_the_terms = lambda x0: jnp.sum(all_gather(x0, 'dp'), 0)  106 us
    psum x1, waiting for transfers between devices, local(): lax.psum(sum_b.astype(jnp.bfloat16), 'dp').astype(jnp.float32)  79.7 us
    all_to_all x4, waiting for transfers between devices, summed_on_arrival(): lax.all_to_all(in_blocks(array, dim, length), axis, 0, 0, tiled=True)  62.8 us
    all_gather x5, waiting for transfers between devices, local(): lax.all_gather(grad_low, 'mp', axis=0, tiled=True)  52.7 us
    all_to_all x5, waiting for transfers between devices, copy_for_each(): return lax.all_to_all(copies, axis, split_axis=0, concat_axis=0, tiled=True)  42.7 us
    ppermute x8, starting transfers between devices, passed_along(): return lax.ppermute(block, axis, route)  30.8 us
    all_to_all x4, waiting for transfers between devices, sent_and_summed(): lax.all_to_all(pieces, axis, split_axis=0, concat_axis=0, tiled=True)  23 us
  transfers between devices with their start and end apart: 28, of which 22 were waited for; matrix products, arithmetic and copies ran while one was open for 27% of the time, Pallas kernels for 0%

profile of v1, /device:TPU:0, one launch (start us, length us, event | category | flops | bytes accessed | tf_op | source)
XLA Modules:
  0.0 895.2 jit_solution(9779160843662902121)
XLA Ops:
  62.2 15.5 %all-to-all-done = f32[4,32,4096]{2,1,0:T(8,128)} async-done(((f32[4,32,4096]{2,1,0:T(8,128)}), f32[4,32,4096]{2,1,0:T(8,128)}, u32[]{:S(2)}, u32[]{:S(2)}) %all-to-all-start) | async-done | bytes 2097184 | tf_op jit(solution)/shard_map/all_to_all | solution.py:23
  90.5 10.4 %all-to-all-done.1 = bf16[4,32,4096]{2,1,0:T(8,128)(2,1)} async-done(((bf16[4,32,4096]{2,1,0:T(8,128)(2,1)}), bf16[4,32,4096]{2,1,0:T(8,128)(2,1)}, u32[]{:S(2)}, u32[]{:S(2)}) %all-to-all-start.1) | async-done | bytes 1048608 | tf_op jit(solution)/shard_map/all_to_all | solution.py:35
  135.3 15.5 %all-to-all-done.2 = f32[4,32,4096]{2,1,0:T(8,128)} async-done(((f32[4,32,4096]{2,1,0:T(8,128)}), f32[4,32,4096]{2,1,0:T(8,128)}, u32[]{:S(2)}, u32[]{:S(2)}) %all-to-all-start.2) | async-done | bytes 2097184 | tf_op jit(solution)/shard_map/all_to_all | solution.py:23
  162.9 7.3 all-to-all-done.3
  170.2 7.3 collective-permute-start.1
  201.7 21.6 %all-to-all-done.4 = f32[4,32,4096]{2,1,0:T(8,128)} async-done(((f32[4,32,4096]{2,1,0:T(8,128)}), f32[4,32,4096]{2,1,0:T(8,128)}, u32[]{:S(2)}, u32[]{:S(2)}) %all-to-all-start.4) | async-done | bytes 2097184 | tf_op jit(solution)/shard_map/all_to_all | solution.py:23
  232.5 11.7 %all-to-all-done.5 = bf16[4,32,4096]{2,1,0:T(8,128)(2,1)} async-done(((bf16[4,32,4096]{2,1,0:T(8,128)(2,1)}), bf16[4,32,4096]{2,1,0:T(8,128)(2,1)}, u32[]{:S(2)}, u32[]{:S(2)}) %all-to-all-start.5) | async-done | bytes 1048608 | tf_op jit(solution)/shard_map/all_to_all | solution.py:35
  244.2 6.5 collective-permute-start.2
  281.5 10.2 %all-to-all-done.6 = f32[4,32,4096]{2,1,0:T(8,128)} async-done(((f32[4,32,4096]{2,1,0:T(8,128)}), f32[4,32,4096]{2,1,0:T(8,128)}, u32[]{:S(2)}, u32[]{:S(2)}) %all-to-all-start.6) | async-done | bytes 2097184 | tf_op jit(solution)/shard_map/all_to_all | solution.py:23
  303.3 8.5 all-to-all-done.7
  311.8 9.2 %collective-permute-start.3 = (bf16[128,4096]{1,0:T(8,128)(2,1)}, bf16[128,4096]{1,0:T(8,128)(2,1)S(1)}, u32[]{:S(2)}, u32[]{:S(2)}) collective-permute-start(bf16[128,4096]{1,0:T(8,128)(2,1)} %bitcast.43), channel_id=1, source_target_pairs={{0,4},{4,8},{8,12},{1,5},{5,9},{9,13},{2,6},{6,10},{10,14},{3,7},{... | collective-permute-start | bytes 3145736 | tf_op jit(solution)/shard_map/ppermute | solution.py:45
  344.9 6.3 fusion.44
  361.5 6.4 convert_bitcast_fusion
  375.8 7.8 collective-permute-done.4
  403.0 12.2 %all-gather.10.cloned.1.call-done = bf16[128,4096]{1,0:T(8,128)(2,1)} async-done(((bf16[32,4096]{1,0:T(8,128)(2,1)}), bf16[128,4096]{1,0:T(8,128)(2,1)}) %all-gather.10.cloned.1.call-update) | async-done | bytes 1048592 | tf_op jit(solution)/shard_map/all_gather | solution.py:213
  431.8 6.5 fusion.40
  454.1 11.5 %all-to-all-done.9 = bf16[4,32,4096]{2,1,0:T(8,128)(2,1)} async-done(((bf16[4,32,4096]{2,1,0:T(8,128)(2,1)}), bf16[4,32,4096]{2,1,0:T(8,128)(2,1)}, u32[]{:S(2)}, u32[]{:S(2)}) %all-to-all-start.9) | async-done | bytes 1048608 | tf_op jit(solution)/shard_map/all_to_all | solution.py:50
  486.7 15.4 %all-gather.12.cloned.1.call-done = bf16[128,4096]{1,0:T(8,128)(2,1)} async-done(((bf16[32,4096]{1,0:T(8,128)(2,1)}), bf16[128,4096]{1,0:T(8,128)(2,1)}) %all-gather.12.cloned.1.call-update) | async-done | bytes 1048592 | tf_op jit(solution)/shard_map/all_gather | solution.py:213
  517.9 6.4 fusion.36
  574.0 8.2 all-gather.14.cloned.1.call-done
  598.9 6.4 fusion.32
  653.0 17.0 %all-gather.16.cloned.1.call-done = bf16[128,4096]{1,0:T(8,128)(2,1)} async-done(((bf16[32,4096]{1,0:T(8,128)(2,1)}), bf16[128,4096]{1,0:T(8,128)(2,1)}) %all-gather.16.cloned.1.call-update) | async-done | bytes 1048592 | tf_op jit(solution)/shard_map/all_gather | solution.py:213
  694.9 79.7 %all-reduce.2.cloned.1.call-done = bf16[1,2,64,256]{3,2,1,0:T(8,128)(2,1)} async-done(((bf16[1,2,64,256]{3,2,1,0:T(8,128)(2,1)}), bf16[1,2,64,256]{3,2,1,0:T(8,128)(2,1)}) %all-reduce.2.cloned.1.call-update) | async-done | bytes 65552 | tf_op jit(solution)/shard_map/psum | solution.py:264
  776.1 105.5 %all-gather.18.cloned.1.call-done = bf16[16,4096,64]{1,2,0:T(8,128)(2,1)} async-done(((bf16[2,4096,64]{1,2,0:T(8,128)(2,1)}), bf16[16,4096,64]{1,2,0:T(8,128)(2,1)}) %all-gather.18.cloned.1.call-update) | async-done | bytes 8388624 | tf_op jit(solution)/shard_map/all_gather | solution.py:261
  (596 shorter events, 465.8 us)
Async XLA Ops:
  7.2 268.2 %all-gather.8.cloned.1.call-start = ((), (), s32[]{:S(2)}) async-start(), calls=%async_computation.13 | async-start | bytes 1310720 | tf_op jit(solution)/shard_map/all_gather | solution.py:213
  45.5 32.2 %all-to-all-start = ((f32[4,32,4096]{2,1,0:T(8,128)}), f32[4,32,4096]{2,1,0:T(8,128)}, u32[]{:S(2)}, u32[]{:S(2)}) async-start(f32[4,32,4096]{2,1,0:T(8,128)} %fusion.20), calls=%async_computation | async-start | bytes 4194304 | tf_op jit(solution)/shard_map/all_to_all | solution.py:23
  82.5 18.5 %all-to-all-start.1 = ((bf16[4,32,4096]{2,1,0:T(8,128)(2,1)}), bf16[4,32,4096]{2,1,0:T(8,128)(2,1)}, u32[]{:S(2)}, u32[]{:S(2)}) async-start(bf16[4,32,4096]{2,1,0:T(8,128)(2,1)} %broadcast_in_dim.169), calls=%async_computation.1 | async-start | bytes 2097152 | tf_op jit(solution)/shard_map/all_to_all | solution.py:35
  124.8 25.9 %all-to-all-start.2 = ((f32[4,32,4096]{2,1,0:T(8,128)}), f32[4,32,4096]{2,1,0:T(8,128)}, u32[]{:S(2)}, u32[]{:S(2)}) async-start(f32[4,32,4096]{2,1,0:T(8,128)} %fusion.18), calls=%async_computation.2 | async-start | bytes 4194304 | tf_op jit(solution)/shard_map/all_to_all | solution.py:23
  154.6 15.7 %all-to-all-start.3 = ((bf16[4,32,4096]{2,1,0:T(8,128)(2,1)}), bf16[4,32,4096]{2,1,0:T(8,128)(2,1)}, u32[]{:S(2)}, u32[]{:S(2)}) async-start(bf16[4,32,4096]{2,1,0:T(8,128)(2,1)} %broadcast_in_dim.171), calls=%async_computation.3 | async-start | bytes 2097152 | tf_op jit(solution)/shard_map/all_to_all | solution.py:35
  170.2 12.2 %collective-permute-start.1 = (bf16[128,4096]{1,0:T(8,128)(2,1)}, bf16[128,4096]{1,0:T(8,128)(2,1)S(1)}, u32[]{:S(2)}, u32[]{:S(2)}) collective-permute-start(bf16[128,4096]{1,0:T(8,128)(2,1)} %bitcast.27), channel_id=1, source_target_pairs={{0,4},{4,8},{8,12},{1,5},{5,9},{9,13},{2,6},{6,10},{10,14},{3,7},{... | collective-permute-start | bytes 3145736 | tf_op jit(solution)/shard_map/ppermute | solution.py:45
  196.9 26.5 %all-to-all-start.4 = ((f32[4,32,4096]{2,1,0:T(8,128)}), f32[4,32,4096]{2,1,0:T(8,128)}, u32[]{:S(2)}, u32[]{:S(2)}) async-start(f32[4,32,4096]{2,1,0:T(8,128)} %fusion.16), calls=%async_computation.4 | async-start | bytes 4194304 | tf_op jit(solution)/shard_map/all_to_all | solution.py:23
  228.2 16.1 %all-to-all-start.5 = ((bf16[4,32,4096]{2,1,0:T(8,128)(2,1)}), bf16[4,32,4096]{2,1,0:T(8,128)(2,1)}, u32[]{:S(2)}, u32[]{:S(2)}) async-start(bf16[4,32,4096]{2,1,0:T(8,128)(2,1)} %broadcast_in_dim.173), calls=%async_computation.5 | async-start | bytes 2097152 | tf_op jit(solution)/shard_map/all_to_all | solution.py:35
  244.2 8.9 collective-permute-start.2
  267.8 23.9 %all-to-all-start.6 = ((f32[4,32,4096]{2,1,0:T(8,128)}), f32[4,32,4096]{2,1,0:T(8,128)}, u32[]{:S(2)}, u32[]{:S(2)}) async-start(f32[4,32,4096]{2,1,0:T(8,128)} %fusion.14), calls=%async_computation.6 | async-start | bytes 4194304 | tf_op jit(solution)/shard_map/all_to_all | solution.py:23
  296.6 15.2 %all-to-all-start.7 = ((bf16[4,32,4096]{2,1,0:T(8,128)(2,1)}), bf16[4,32,4096]{2,1,0:T(8,128)(2,1)}, u32[]{:S(2)}, u32[]{:S(2)}) async-start(bf16[4,32,4096]{2,1,0:T(8,128)(2,1)} %broadcast_in_dim.175), calls=%async_computation.7 | async-start | bytes 2097152 | tf_op jit(solution)/shard_map/all_to_all | solution.py:35
  311.8 14.7 %collective-permute-start.3 = (bf16[128,4096]{1,0:T(8,128)(2,1)}, bf16[128,4096]{1,0:T(8,128)(2,1)S(1)}, u32[]{:S(2)}, u32[]{:S(2)}) collective-permute-start(bf16[128,4096]{1,0:T(8,128)(2,1)} %bitcast.43), channel_id=1, source_target_pairs={{0,4},{4,8},{8,12},{1,5},{5,9},{9,13},{2,6},{6,10},{10,14},{3,7},{... | collective-permute-start | bytes 3145736 | tf_op jit(solution)/shard_map/ppermute | solution.py:45
  355.9 14.4 %all-to-all-start.8 = ((bf16[4,32,4096]{2,1,0:T(8,128)(2,1)}), bf16[4,32,4096]{2,1,0:T(8,128)(2,1)S(1)}, u32[]{:S(2)}, u32[]{:S(2)}) async-start(bf16[4,32,4096]{2,1,0:T(8,128)(2,1)} %bitcast.1219), calls=%async_computation.8 | async-start | bytes 2097152 | tf_op jit(solution)/shard_map/all_to_all | solution.py:50
  359.4 55.7 %all-gather.10.cloned.1.call-start = ((), (), s32[]{:S(2)}) async-start(), calls=%async_computation.14 | async-start | bytes 1310720 | tf_op jit(solution)/shard_map/all_gather | solution.py:213
  373.1 10.5 %collective-permute-start.4 = (bf16[32,4096]{1,0:T(8,128)(2,1)S(1)}, bf16[32,4096]{1,0:T(8,128)(2,1)S(1)}, u32[]{:S(2)}, u32[]{:S(2)}) collective-permute-start(bf16[32,4096]{1,0:T(8,128)(2,1)S(1)} %fusion.489), channel_id=1, source_target_pairs={{4,0},{8,4},{12,8},{5,1},{9,5},{13,9},{6,2},{10,6},{14,10},{7,3},{... | collective-permute-start | bytes 786440 | tf_op jit(solution)/shard_map/ppermute | solution.py:45
  447.9 17.7 %all-to-all-start.9 = ((bf16[4,32,4096]{2,1,0:T(8,128)(2,1)}), bf16[4,32,4096]{2,1,0:T(8,128)(2,1)}, u32[]{:S(2)}, u32[]{:S(2)}) async-start(bf16[4,32,4096]{2,1,0:T(8,128)(2,1)} %bitcast.1220), calls=%async_computation.9 | async-start | bytes 2097152 | tf_op jit(solution)/shard_map/all_to_all | solution.py:50
  452.3 49.8 %all-gather.12.cloned.1.call-start = ((), (), s32[]{:S(2)}) async-start(), calls=%async_computation.15 | async-start | bytes 1310720 | tf_op jit(solution)/shard_map/all_gather | solution.py:213
  529.1 17.6 %all-to-all-start.10 = ((bf16[4,32,4096]{2,1,0:T(8,128)(2,1)}), bf16[4,32,4096]{2,1,0:T(8,128)(2,1)}, u32[]{:S(2)}, u32[]{:S(2)}) async-start(bf16[4,32,4096]{2,1,0:T(8,128)(2,1)} %bitcast.1218), calls=%async_computation.10 | async-start | bytes 2097152 | tf_op jit(solution)/shard_map/all_to_all | solution.py:50
  533.3 48.9 %all-gather.14.cloned.1.call-start = ((), (), s32[]{:S(2)}) async-start(), calls=%async_computation.16 | async-start | bytes 1310720 | tf_op jit(solution)/shard_map/all_gather | solution.py:213
  614.9 17.6 %all-to-all-start.11 = ((bf16[4,32,4096]{2,1,0:T(8,128)(2,1)}), bf16[4,32,4096]{2,1,0:T(8,128)(2,1)}, u32[]{:S(2)}, u32[]{:S(2)}) async-start(bf16[4,32,4096]{2,1,0:T(8,128)(2,1)} %bitcast.1217), calls=%async_computation.11 | async-start | bytes 2097152 | tf_op jit(solution)/shard_map/all_to_all | solution.py:50
  619.2 50.8 %all-gather.16.cloned.1.call-start = ((), (), s32[]{:S(2)}) async-start(), calls=%async_computation.17 | async-start | bytes 1310720 | tf_op jit(solution)/shard_map/all_gather | solution.py:213
  682.2 9.2 %all-to-all-start.12 = ((f32[4,1,4096]{2,1,0:T(1,128)}), f32[4,1,4096]{2,1,0:T(1,128)S(1)}, u32[]{:S(2)}, u32[]{:S(2)}) async-start(f32[4,1,4096]{2,1,0:T(1,128)} %reshape.1704), calls=%async_computation.12 | async-start | bytes 131072 | tf_op jit(solution)/shard_map/all_to_all | solution.py:35
  685.8 88.8 %all-reduce.2.cloned.1.call-start = ((), (), s32[]{:S(2)}) async-start(), calls=%async_computation.18 | async-start | bytes 131072 | tf_op jit(solution)/shard_map/psum | solution.py:264
  686.6 195.1 %all-gather.18.cloned.1.call-start = ((), (), s32[]{:S(2)}) async-start(), calls=%async_computation.19 | async-start | bytes 9437184 | tf_op jit(solution)/shard_map/all_gather | solution.py:261
  (123 other events, 696.0 us)
Sparse Core Ops, SparseCore 0:
  11.1 26.9 all-gather.7
  385.2 29.8 all-gather.9
  474.8 27.2 all-gather.11
  555.6 26.6 all-gather.13
  643.7 26.3 all-gather.15
  688.8 85.7 all-reduce.1
  777.5 104.0 all-gather.17
